TPU v7x, 32 devices: a whole 2x2x4 slice. The times are simulated.
32 devices in a mesh: morton: 8 (over y, x, core), sub: 4 (over z).
Axes of the slice: x: 2, y: 2, z: 4, core: 2. Of those that a mesh axis runs over, the one named last changes fastest.
Arguments:
- leaf_dens: bfloat16 [512, 8, 294], P(('morton', 'sub')), may hold values from -6 to 6
- leaf_sources: int32 [512, 189], P(('morton', 'sub')), may hold values from 0 to 191, as said below
- leaf_classes: int32 [512, 189], P(('morton', 'sub')), may hold values from 0 to 15
- grand_sources: int32 [8, 189], P('morton'), may hold values from 0 to 7
- grand_classes: int32 [8, 189], P('morton'), may hold values from 0 to 15
- up_ops: bfloat16 [8, 294, 294], replicated, may hold values from -0.125 to 0.125
- far_ops: bfloat16 [16, 294, 294], replicated, may hold values from -0.02734375 to 0.02734375
- down_ops: bfloat16 [8, 294, 294], replicated, may hold values from -0.375 to 0.375
Outputs:
- leaf_local: bfloat16 [512, 8, 294], P(('morton', 'sub'))
Inputs may be any that keep to these rules, and one draw needn't show every extreme that they name: `leaf_sources`: positions in the pool of the finest octants of three Morton ranges of 64 octants each (range t // 64 - 1, its own, and the next); rows of the first range never name the range before it and rows of the last never name the range after it.
All inputs are finite; a program needn't handle non-finite values.
Results may differ from a plain program's by a relative error of at most 0.0085.
Values may be sent and summed in bfloat16 or wider, within the bound.
No kernel may reach another device: no remote copies, remote signals or barrier semaphores. Data moves between devices by JAX's collectives and lax.ppermute only.
A program may use at most 64 MiB of HBM per device.

v0:
```python
import jax
import jax.numpy as jnp
from jax import lax
from jax.sharding import PartitionSpec as P


def from_partner(value, axis, distance):
    mask = 2**distance
    pairs = [(source, source ^ mask) for source in range(lax.axis_size(axis))]
    return lax.ppermute(value, axis, pairs)


def padded(cells, sides, width):
    for axis, dim in sides:
        count = lax.axis_size(axis)
        ends = count - 1
        head = lax.slice_in_dim(cells, 0, width, axis=dim)
        tail = lax.slice_in_dim(cells, cells.shape[dim] - width, cells.shape[dim], axis=dim)
        cells = jnp.concatenate(
            [
                lax.ppermute(tail, axis, [(i, (i + 1) % count) for i in range(ends)]),
                cells,
                lax.ppermute(head, axis, [((i + 1) % count, i) for i in range(ends)]),
            ],
            axis=dim,
        )
    return cells


def far_block(pool_rows, sources, classes, far_matrix, rhs_count, width):
    targets = sources.shape[0]
    classes_count = far_matrix.shape[0] // width
    pool_size = pool_rows.shape[0]
    source_hot = (
        sources[:, :, None] == jnp.arange(pool_size, dtype=jnp.int32)[None, None, :]
    ).astype(jnp.bfloat16)
    class_hot = (
        classes[:, :, None] == jnp.arange(classes_count, dtype=jnp.int32)[None, None, :]
    ).astype(jnp.bfloat16)
    counts = jnp.einsum(
        "tec,teq->tcq", class_hot, source_hot, preferred_element_type=jnp.float32
    ).astype(jnp.bfloat16)
    aggregate = jnp.dot(
        counts.reshape(targets * classes_count, pool_size),
        pool_rows,
        preferred_element_type=jnp.float32,
    ).astype(jnp.bfloat16)
    rows_in = aggregate.reshape(targets, classes_count, rhs_count, width).transpose(0, 2, 1, 3)
    rows_in = rows_in.reshape(targets * rhs_count, classes_count * width)
    return jnp.dot(rows_in, far_matrix, preferred_element_type=jnp.float32).reshape(
        targets, rhs_count, width
    )


def shards(
    leaf_dens, leaf_sources, leaf_classes, grand_sources, grand_classes, up_ops, far_ops, down_ops
):
    own_leaves, rhs_count, width = leaf_dens.shape
    classes_count = far_ops.shape[0]
    parents_here = own_leaves // 8
    grand_span = 64 // own_leaves
    sub_index = lax.axis_index("sub")
    position = sub_index % grand_span
    children = leaf_dens.reshape(parents_here, 8, rhs_count, width)
    parent_dens = jnp.einsum(
        "jknw,kwv->jnv", children, up_ops, preferred_element_type=jnp.float32
    ).astype(jnp.bfloat16)
    mine = parent_dens
    for bit_number in range(grand_span.bit_length() - 1):
        partner = from_partner(mine, "sub", bit_number)
        lower_half = sub_index // (1 << bit_number) % 2 == 0
        mine = jnp.where(
            lower_half,
            jnp.concatenate([mine, partner], axis=0),
            jnp.concatenate([partner, mine], axis=0),
        )
    grand_dens = jnp.einsum("knw,kwv->nv", mine, up_ops, preferred_element_type=jnp.float32).astype(
        jnp.bfloat16
    )
    flat_dens = grand_dens.reshape(rhs_count * width)
    piece_len = rhs_count * width // grand_span
    piece = lax.dynamic_slice_in_dim(flat_dens, position * piece_len, piece_len, 0)
    range_pieces = lax.all_gather(piece[None], "sub", axis=0, tiled=True)
    range_dens = range_pieces.reshape(range_pieces.shape[0] // grand_span, rhs_count * width)
    grand_pool = lax.all_gather(range_dens, "morton", axis=0, tiled=True)
    far_matrix = far_ops.reshape(classes_count * width, width)
    row_pick = sub_index // grand_span
    my_sources = lax.dynamic_slice_in_dim(grand_sources, row_pick, 1, 0)[0]
    my_classes = lax.dynamic_slice_in_dim(grand_classes, row_pick, 1, 0)[0]
    grand_count = grand_pool.shape[0]
    source_hot = (my_sources[:, None] == jnp.arange(grand_count, dtype=jnp.int32)[None, :]).astype(
        jnp.bfloat16
    )
    class_hot = (my_classes[:, None] == jnp.arange(classes_count, dtype=jnp.int32)[None, :]).astype(
        jnp.bfloat16
    )
    grand_counts = jnp.dot(class_hot.T, source_hot, preferred_element_type=jnp.float32).astype(
        jnp.bfloat16
    )
    grand_agg = jnp.dot(grand_counts, grand_pool, preferred_element_type=jnp.float32).astype(
        jnp.bfloat16
    )
    grand_rows = grand_agg.reshape(classes_count, rhs_count, width).transpose(1, 0, 2)
    grand_rows = grand_rows.reshape(rhs_count, classes_count * width)
    grand_local = jnp.dot(grand_rows, far_matrix, preferred_element_type=jnp.float32).astype(
        jnp.bfloat16
    )
    parent_ops = lax.dynamic_slice_in_dim(down_ops, position * parents_here, parents_here, 0)
    parent_local = jnp.einsum(
        "nw,jwv->jnv", grand_local, parent_ops, preferred_element_type=jnp.float32
    ).astype(jnp.bfloat16)
    range_leaves = lax.all_gather(leaf_dens, "sub", axis=0, tiled=True)
    leaf_pool = padded(range_leaves, (("morton", 0),), range_leaves.shape[0])
    pool_rows = leaf_pool.reshape(leaf_pool.shape[0], rhs_count * width)
    leaf_far = far_block(pool_rows, leaf_sources, leaf_classes, far_matrix, rhs_count, width)
    downward = jnp.einsum(
        "jnw,kwv->jknv", parent_local, down_ops, preferred_element_type=jnp.float32
    )
    downward = downward.reshape(own_leaves, rhs_count, width)
    return (leaf_far + downward).astype(jnp.bfloat16)


def solution(mesh):
    placed = (
        P(("morton", "sub"), None, None),
        P(("morton", "sub"), None),
        P(("morton", "sub"), None),
        P("morton", None),
        P("morton", None),
        P(),
        P(),
        P(),
    )
    return jax.shard_map(
        shards,
        mesh=mesh,
        in_specs=placed,
        out_specs=P(("morton", "sub"), None, None),
        check_vma=False,
    )
```

profile of v0, /device:TPU:0, one launch (start us, length us, event | category | flops | bytes accessed | tf_op | source)
XLA Modules:
  0.0 82.7 jit_solution(12412377823219016353)
XLA Ops:
  0.0 2.0 %fusion.34 = bf16[2,8,294]{2,1,0:T(8,128)(2,1)S(1)} fusion(bf16[2,8,8,294]{3,2,1,0:T(8,128)(2,1)} %bitcast.77, bf16[8,294,294]{2,0,1:T(8,128)(2,1)} %param.13), kind=kOutput, calls=%fused_computation.25 | convolution fusion | flops 22132320 | bytes 1467648 | tf_op jit(solution)/shard_map/jknw,kwv->jnv/dot_general | solution.py:65
  2.0 3.2 %collective-permute-start.2 = (bf16[2,8,294]{2,1,0:T(8,128)(2,1)S(1)}, bf16[2,8,294]{2,1,0:T(8,128)(2,1)S(1)}, u32[]{:S(2)}, u32[]{:S(2)}) collective-permute-start(bf16[2,8,294]{2,1,0:T(8,128)(2,1)S(1)} %fusion.34), channel_id=1, source_target_pairs={{0,1},{1,0},{2,3},{3,2},{4,5},{5,4},{6,7},{7,6},{8,9},{9,8},{10,11... | collective-permute-start | bytes 28232 | tf_op jit(solution)/shard_map/ppermute | solution.py:10
  5.2 14.6 %all_gather.9 = bf16[64,8,294]{2,1,0:T(8,128)(2,1)S(1)} all-gather(bf16[16,8,294]{2,1,0:T(8,128)(2,1)S(1)} %copy-done), channel_id=1, replica_groups=mesh['morton'=8,'sub'=4] {'sub'}, dimensions={0}, use_global_device_ids=true | all-gather | bytes 376320 | tf_op jit(solution)/shard_map/all_gather | solution.py:112
  19.8 1.3 %collective-permute-start = (bf16[64,8,294]{2,1,0:T(8,128)(2,1)S(1)}, bf16[64,8,294]{2,1,0:T(8,128)(2,1)S(1)}, u32[]{:S(2)}, u32[]{:S(2)}) collective-permute-start(bf16[64,8,294]{2,1,0:T(8,128)(2,1)S(1)} %all_gather.9), channel_id=1, source_target_pairs={{0,4},{4,8},{8,12},{12,16},{16,20},{20,24},{24,28},{1,5},{5,9},{9,... | collective-permute-start | bytes 903176 | tf_op jit(solution)/shard_map/ppermute | solution.py:21
  21.1 1.3 %collective-permute-start.1 = (bf16[64,8,294]{2,1,0:T(8,128)(2,1)S(1)}, bf16[64,8,294]{2,1,0:T(8,128)(2,1)S(1)}, u32[]{:S(2)}, u32[]{:S(2)}) collective-permute-start(bf16[64,8,294]{2,1,0:T(8,128)(2,1)S(1)} %all_gather.9), channel_id=1, source_target_pairs={{4,0},{8,4},{12,8},{16,12},{20,16},{24,20},{28,24},{5,1},{9,5},{13... | collective-permute-start | bytes 903176 | tf_op jit(solution)/shard_map/ppermute | solution.py:23
  22.5 0.0 collective-permute-done.2
  22.5 0.8 collective-permute-start.3
  23.3 1.5 %fusion.20 = bf16[16,16,192]{2,1,0:T(8,128)(2,1)} fusion(s32[16,189]{1,0:T(8,128)S(1)} %copy-done.1, s32[16,189]{1,0:T(8,128)S(1)} %copy-done.2), kind=kOutput, calls=%fused_computation.20 | convolution fusion | flops 19257600 | bytes 122496 | tf_op jit(solution)/shard_map/tec,teq->tcq/dot_general | solution.py:40
  24.7 0.6 dynamic-slice
  25.3 0.6 dynamic-slice.1
  25.9 1.7 %copy.21 = bf16[8,294,294]{2,1,0:T(8,128)(2,1)S(1)} copy(bf16[8,294,294]{2,0,1:T(8,128)(2,1)} %param.15) | data formatting | bytes 2765952 | tf_op args[7]
  27.6 0.0 copy-start.3
  27.7 0.0 copy-start.4
  28.9 0.0 collective-permute-done.3
  28.9 1.9 %fusion.47 = bf16[8,294]{1,0:T(8,128)(2,1)S(1)} fusion(bf16[8,294,294]{2,0,1:T(8,128)(2,1)} %param.13, bf16[4,8,294]{2,1,0:T(8,128)(2,1)S(1)} %collective-permute-done.3, bf16[4,8,294]{2,1,0:T(8,128)(2,1)S(1)} %maximum_select_fusion.2, pred[]{:T(512)S(6)} %eq.80), kind=kOutput, calls=%fused_computation.30 | convolution fusion | flops 11122608 | bytes 1425313 | tf_op jit(solution)/shard_map/knw,kwv->nv/dot_general | solution.py:77
  30.8 0.1 reshape.38
  30.9 0.1 dynamic_slice.9
  31.0 0.2 dynamic-update-slice
  31.2 11.4 %all-reduce = bf16[2352]{0:T(1024)(128)(2,1)S(1)} all-reduce(bf16[2352]{0:T(1024)(128)(2,1)S(1)} %dynamic-update-slice), channel_id=2, replica_groups=mesh['morton'=8,'sub'=4] {'sub'}, use_global_device_ids=true, to_apply=%add | all-reduce | flops 2352 | bytes 9408
  42.6 0.3 dynamic-update-slice.1
  42.9 25.5 %all-reduce.1 = bf16[18816]{0:T(1024)(128)(2,1)S(1)} all-reduce(bf16[18816]{0:T(1024)(128)(2,1)S(1)} %dynamic-update-slice.1), channel_id=3, replica_groups=mesh['morton'=8,'sub'=4] {'morton'}, use_global_device_ids=true, to_apply=%add.1 | all-reduce | flops 18816 | bytes 75264
  68.4 0.1 reshape.44
  68.6 0.5 convolution_convert_fusion.1
  69.0 0.2 reshape.40
  69.2 3.0 %fusion.50 = bf16[8,294,1]{1,0,2:T(8,128)(2,1)S(1)} fusion(bf16[16,294,294]{2,0,1:T(8,128)(2,1)} %param.14, bf16[16,8,294]{2,1,0:T(8,128)(2,1)S(1)} %reshape.40), kind=kOutput, calls=%fused_computation.31 | convolution fusion | flops 22129968 | bytes 2845920 | tf_op jit(solution)/shard_map/dot_general | solution.py:105
  72.3 0.6 fusion.6
  72.8 0.2 pad_maximum_fusion
  73.1 0.9 %reshape.35 = bf16[192,2352]{1,0:T(8,128)(2,1)S(1)} reshape(bf16[192,8,294]{2,1,0:T(8,128)(2,1)S(1)} %pad_maximum_fusion) | data formatting | bytes 1806336 | tf_op jit(solution)/shard_map/reshape | solution.py:114
  74.0 1.5 %convolution_convert_fusion = bf16[256,2352]{0,1:T(8,128)(2,1)S(1)} fusion(bf16[256,192]{1,0:T(8,128)(2,1)} %bitcast.79, bf16[192,2352]{1,0:T(8,128)(2,1)S(1)} %reshape.35), kind=kOutput, calls=%fused_computation | convolution fusion | flops 231813120 | bytes 2205696 | tf_op jit(solution)/shard_map/dot_general | solution.py:43
  75.5 0.8 %copy.19 = bf16[256,2352]{1,0:T(8,128)(2,1)S(1)} copy(bf16[256,2352]{0,1:T(8,128)(2,1)S(1)} %convolution_convert_fusion) | data formatting | bytes 2408448 | tf_op jit(solution)/shard_map/convert_element_type | solution.py:47
  76.4 2.0 %reshape.36 = bf16[16,16,8,294]{3,2,1,0:T(8,128)(2,1)S(1)} reshape(bf16[256,2352]{1,0:T(8,128)(2,1)S(1)} %copy.19) | data formatting | bytes 2408448 | tf_op jit(solution)/shard_map/reshape | solution.py:48
  78.3 4.4 %fusion.26 = bf16[16,8,294]{2,1,0:T(8,128)(2,1)} fusion(f32[16,8,294]{2,1,0:T(8,128)S(1)} %bitcast.78, bf16[16,294,294]{2,0,1:T(8,128)(2,1)} %param.14, bf16[16,16,8,294]{3,2,1,0:T(8,128)(2,1)S(1)} %reshape.36), kind=kOutput, calls=%fused_computation.22 | convolution fusion | flops 354117120 | bytes 4195968 | tf_op jit(solution)/shard_map/dot_general | solution.py:50
  (17 shorter events, 0.1 us)
Async XLA Ops:
  0.0 24.7 %copy-start.6 = (u32[32]{0:T(128)S(1)}, u32[32]{0:T(128)}, u32[]{:S(2)}) copy-start(u32[32]{0:T(128)} %constant.71) | copy-start | bytes 388
  0.0 25.3 %copy-start.5 = (u32[32]{0:T(128)S(1)}, u32[32]{0:T(128)}, u32[]{:S(2)}) copy-start(u32[32]{0:T(128)} %constant.76) | copy-start | bytes 388
  0.0 5.2 %copy-start = (bf16[16,8,294]{2,1,0:T(8,128)(2,1)S(1)}, bf16[16,8,294]{2,1,0:T(8,128)(2,1)}, u32[]{:S(2)}) copy-start(bf16[16,8,294]{2,1,0:T(8,128)(2,1)} %param.8) | copy-start | bytes 225796
  0.0 23.2 %copy-start.2 = (s32[16,189]{1,0:T(8,128)S(1)}, s32[16,189]{1,0:T(8,128)}, u32[]{:S(2)}) copy-start(s32[16,189]{1,0:T(8,128)} %param.10) | copy-start | bytes 36292
  0.0 23.2 %copy-start.1 = (s32[16,189]{1,0:T(8,128)S(1)}, s32[16,189]{1,0:T(8,128)}, u32[]{:S(2)}) copy-start(s32[16,189]{1,0:T(8,128)} %param.9) | copy-start | bytes 36292
  2.0 20.4 %collective-permute-start.2 = (bf16[2,8,294]{2,1,0:T(8,128)(2,1)S(1)}, bf16[2,8,294]{2,1,0:T(8,128)(2,1)S(1)}, u32[]{:S(2)}, u32[]{:S(2)}) collective-permute-start(bf16[2,8,294]{2,1,0:T(8,128)(2,1)S(1)} %fusion.34), channel_id=1, source_target_pairs={{0,1},{1,0},{2,3},{3,2},{4,5},{5,4},{6,7},{7,6},{8,9},{9,8},{10,11... | collective-permute-start | bytes 28232 | tf_op jit(solution)/shard_map/ppermute | solution.py:10
  19.8 53.0 %collective-permute-start = (bf16[64,8,294]{2,1,0:T(8,128)(2,1)S(1)}, bf16[64,8,294]{2,1,0:T(8,128)(2,1)S(1)}, u32[]{:S(2)}, u32[]{:S(2)}) collective-permute-start(bf16[64,8,294]{2,1,0:T(8,128)(2,1)S(1)} %all_gather.9), channel_id=1, source_target_pairs={{0,4},{4,8},{8,12},{12,16},{16,20},{20,24},{24,28},{1,5},{5,9},{9,... | collective-permute-start | bytes 903176 | tf_op jit(solution)/shard_map/ppermute | solution.py:21
  21.1 51.7 %collective-permute-start.1 = (bf16[64,8,294]{2,1,0:T(8,128)(2,1)S(1)}, bf16[64,8,294]{2,1,0:T(8,128)(2,1)S(1)}, u32[]{:S(2)}, u32[]{:S(2)}) collective-permute-start(bf16[64,8,294]{2,1,0:T(8,128)(2,1)S(1)} %all_gather.9), channel_id=1, source_target_pairs={{4,0},{8,4},{12,8},{16,12},{20,16},{24,20},{28,24},{5,1},{9,5},{13... | collective-permute-start | bytes 903176 | tf_op jit(solution)/shard_map/ppermute | solution.py:23
  22.5 6.4 %collective-permute-start.3 = (bf16[4,8,294]{2,1,0:T(8,128)(2,1)S(1)}, bf16[4,8,294]{2,1,0:T(8,128)(2,1)S(1)}, u32[]{:S(2)}, u32[]{:S(2)}) collective-permute-start(bf16[4,8,294]{2,1,0:T(8,128)(2,1)S(1)} %maximum_select_fusion.2), channel_id=1, source_target_pairs={{0,2},{1,3},{2,0},{3,1},{4,6},{5,7},{6,4},{7,5},{8,10},{9,11},{10,... | collective-permute-start | bytes 56456 | tf_op jit(solution)/shard_map/ppermute | solution.py:10
  27.6 40.9 %copy-start.3 = (s32[1,189]{1,0:T(1,128)S(1)}, s32[1,189]{1,0:T(1,128)}, u32[]{:S(2)}) copy-start(s32[1,189]{1,0:T(1,128)} %param.11) | copy-start | bytes 2272
  27.7 40.9 %copy-start.4 = (s32[1,189]{1,0:T(1,128)S(1)}, s32[1,189]{1,0:T(1,128)}, u32[]{:S(2)}) copy-start(s32[1,189]{1,0:T(1,128)} %param.12) | copy-start | bytes 2272
where the time goes:
time: 83.1 us; the launch traced here: 82.7 us
  blocking collectives  51.5 us (62%)
  matrix products  15.4 us (19%)
  local copies, waits for them, and re-layouts  7.59 us (9%)
  starting transfers between devices  6.51 us (8%)
  between operations  1.42 us (2%)
    unnamed x2, blocking collectives  36.9 us
    all_gather x1, blocking collectives, shards(): range_leaves = lax.all_gather(leaf_dens, 'sub', axis=0, tiled=True)  14.6 us
    dot_general x1, matrix products, far_block(): jnp.dot(rows_in, far_matrix, preferred_element_type=jnp.float32)  4.39 us
    ppermute x2, starting transfers between devices, from_partner(): return lax.ppermute(value, axis, pairs)  3.91 us
    unnamed x21, local copies, waits for them, and re-layouts  3.43 us
    dot_general x1, matrix products, shards(): jnp.dot(grand_rows, far_matrix, preferred_element_type=jnp.float32)  3.05 us
    dot_general x1, matrix products, shards(): jnp.einsum('jknw,kwv->jnv', children, up_ops, preferred_element_type=jnp....  2.02 us
    reshape x1, local copies, waits for them, and re-layouts, far_block(): aggregate.reshape(targets, classes_count, rhs_count, width)  1.96 us
  transfers between devices with their start and end apart: 4, of which 0 were waited for; matrix products, arithmetic and copies ran while one was open for 14% of the time, Pallas kernels for 0%

commit v1 on v0

--- a/solution.py
+++ b/solution.py
@@ -109,7 +109,8 @@
     parent_local = jnp.einsum(
         "nw,jwv->jnv", grand_local, parent_ops, preferred_element_type=jnp.float32
     ).astype(jnp.bfloat16)
-    range_leaves = lax.all_gather(leaf_dens, "sub", axis=0, tiled=True)
+    outgoing = jnp.stack([leaf_dens] * lax.axis_size("sub"))
+    range_leaves = jnp.concatenate(lax.all_to_all(outgoing, "sub", 0, 0), axis=0)
     leaf_pool = padded(range_leaves, (("morton", 0),), range_leaves.shape[0])
     pool_rows = leaf_pool.reshape(leaf_pool.shape[0], rhs_count * width)
     leaf_far = far_block(pool_rows, leaf_sources, leaf_classes, far_matrix, rhs_count, width)

time: 83.1 us -> 78 us (0.939)
  the two profiles are of different devices: /device:TPU:0 before, /device:TPU:6 now
where the time goes in v1:
time: 78 us; the launch traced here: 77.7 us
  blocking collectives  30 us (38%)
  matrix products  15.3 us (20%)
  starting transfers between devices  13 us (17%)
  waiting for transfers between devices  10.7 us (14%)
  local copies, waits for them, and re-layouts  7.15 us (9%)
  between operations  1.49 us (2%)
    unnamed x2, blocking collectives  30 us
    ppermute x1, waiting for transfers between devices, padded(): lax.ppermute(tail, axis, [(i, (i + 1) % count) for i in range(ends)])  5.68 us
    ppermute x2, waiting for transfers between devices, from_partner(): return lax.ppermute(value, axis, pairs)  5.01 us
    ppermute x2, starting transfers between devices, from_partner(): return lax.ppermute(value, axis, pairs)  4.62 us
    dot_general x1, matrix products, far_block(): jnp.dot(rows_in, far_matrix, preferred_element_type=jnp.float32)  4.41 us
    all_to_all x1, starting transfers between devices, shards(): lax.all_to_all(outgoing, 'sub', 0, 0)  3.86 us
    dot_general x1, matrix products, shards(): jnp.dot(grand_rows, far_matrix, preferred_element_type=jnp.float32)  3.05 us
    ppermute x1, starting transfers between devices, padded(): lax.ppermute(head, axis, [((i + 1) % count, i) for i in range(ends)])  2.59 us
  transfers between devices with their start and end apart: 5, of which 2 were waited for; matrix products, arithmetic and copies ran while one was open for 16% of the time, Pallas kernels for 0%

profile of v1, /device:TPU:6, one launch (start us, length us, event | category | flops | bytes accessed | tf_op | source)
XLA Modules:
  0.0 77.7 jit_solution(5580416774912332954)
XLA Ops:
  0.0 2.1 %fusion.35 = bf16[2,8,294]{2,1,0:T(8,128)(2,1)S(1)} fusion(bf16[2,8,8,294]{3,2,1,0:T(8,128)(2,1)} %bitcast.81, bf16[8,294,294]{2,0,1:T(8,128)(2,1)} %param.13), kind=kOutput, calls=%fused_computation.25 | convolution fusion | flops 22132320 | bytes 1467648 | tf_op jit(solution)/shard_map/jknw,kwv->jnv/dot_general | solution.py:65
  2.1 1.6 %collective-permute-start.2 = (bf16[2,8,294]{2,1,0:T(8,128)(2,1)S(1)}, bf16[2,8,294]{2,1,0:T(8,128)(2,1)S(1)}, u32[]{:S(2)}, u32[]{:S(2)}) collective-permute-start(bf16[2,8,294]{2,1,0:T(8,128)(2,1)S(1)} %fusion.35), channel_id=1, source_target_pairs={{0,1},{1,0},{2,3},{3,2},{4,5},{5,4},{6,7},{7,6},{8,9},{9,8},{10,11... | collective-permute-start | bytes 28232 | tf_op jit(solution)/shard_map/ppermute | solution.py:10
  3.8 0.8 %stack.2 = bf16[4,16,8,294]{3,2,1,0:T(8,128)(2,1)} broadcast(bf16[16,8,294]{2,1,0:T(8,128)(2,1)S(1)} %copy-done.1), dimensions={1,2,3} | broadcast | bytes 376320 | tf_op jit(solution)/shard_map/stack | solution.py:112
  4.6 3.9 %all-to-all-start = ((bf16[4,16,8,294]{3,2,1,0:T(8,128)(2,1)}), bf16[4,16,8,294]{3,2,1,0:T(8,128)(2,1)S(1)}, u32[]{:S(2)}, u32[]{:S(2)}) async-start(bf16[4,16,8,294]{3,2,1,0:T(8,128)(2,1)} %stack.2), calls=%async_computation | async-start | bytes 786432 | tf_op jit(solution)/shard_map/all_to_all | solution.py:113
  8.4 1.5 %fusion.21 = bf16[16,16,192]{2,1,0:T(8,128)(2,1)} fusion(s32[16,189]{1,0:T(8,128)S(1)} %copy-done.3, s32[16,189]{1,0:T(8,128)S(1)} %copy-done.4), kind=kOutput, calls=%fused_computation.20 | convolution fusion | flops 19257600 | bytes 122496 | tf_op jit(solution)/shard_map/tec,teq->tcq/dot_general | solution.py:40
  10.0 3.0 %collective-permute-start.3 = (bf16[4,8,294]{2,1,0:T(8,128)(2,1)S(1)}, bf16[4,8,294]{2,1,0:T(8,128)(2,1)S(1)}, u32[]{:S(2)}, u32[]{:S(2)}) collective-permute-start(bf16[4,8,294]{2,1,0:T(8,128)(2,1)S(1)} %maximum_select_fusion.2), channel_id=1, source_target_pairs={{0,2},{1,3},{2,0},{3,1},{4,6},{5,7},{6,4},{7,5},{8,10},{9,11},{10,... | collective-permute-start | bytes 56456 | tf_op jit(solution)/shard_map/ppermute | solution.py:10
  12.9 0.5 constant_dynamic-slice_fusion
  13.5 0.6 dynamic-slice.1
  14.1 0.6 dynamic-slice
  15.9 5.0 %collective-permute-done.3 = bf16[4,8,294]{2,1,0:T(8,128)(2,1)S(1)} collective-permute-done((bf16[4,8,294]{2,1,0:T(8,128)(2,1)S(1)}, bf16[4,8,294]{2,1,0:T(8,128)(2,1)S(1)}, u32[]{:S(2)}, u32[]{:S(2)}) %collective-permute-start.3) | collective-permute-done | bytes 18848 | tf_op jit(solution)/shard_map/ppermute | solution.py:10
  20.9 1.9 %fusion.48 = bf16[8,294]{1,0:T(8,128)(2,1)S(1)} fusion(bf16[8,294,294]{2,0,1:T(8,128)(2,1)} %param.13, bf16[4,8,294]{2,1,0:T(8,128)(2,1)S(1)} %collective-permute-done.3, bf16[4,8,294]{2,1,0:T(8,128)(2,1)S(1)} %maximum_select_fusion.2, pred[]{:T(512)S(6)} %eq.80), kind=kOutput, calls=%fused_computation.30 | convolution fusion | flops 11122608 | bytes 1425313 | tf_op jit(solution)/shard_map/knw,kwv->nv/dot_general | solution.py:77
  22.8 0.1 reshape.45
  22.9 0.1 dynamic_slice.9
  23.0 0.2 dynamic-update-slice
  23.2 9.9 %all-reduce = bf16[2352]{0:T(1024)(128)(2,1)S(1)} all-reduce(bf16[2352]{0:T(1024)(128)(2,1)S(1)} %dynamic-update-slice), channel_id=2, replica_groups=mesh['morton'=8,'sub'=4] {'sub'}, use_global_device_ids=true, to_apply=%add | all-reduce | flops 2352 | bytes 9408
  33.2 0.3 dynamic-update-slice.1
  33.5 20.1 %all-reduce.1 = bf16[18816]{0:T(1024)(128)(2,1)S(1)} all-reduce(bf16[18816]{0:T(1024)(128)(2,1)S(1)} %dynamic-update-slice.1), channel_id=3, replica_groups=mesh['morton'=8,'sub'=4] {'morton'}, use_global_device_ids=true, to_apply=%add.1 | all-reduce | flops 18816 | bytes 75264
  53.6 0.1 reshape.51
  53.7 0.4 convolution_convert_fusion.1
  54.1 0.2 reshape.47
  54.3 2.6 %collective-permute-start.1 = (bf16[64,8,294]{2,1,0:T(8,128)(2,1)S(1)}, bf16[64,8,294]{2,1,0:T(8,128)(2,1)S(1)}, u32[]{:S(2)}, u32[]{:S(2)}) collective-permute-start(bf16[64,8,294]{2,1,0:T(8,128)(2,1)S(1)} %bitcast.79), channel_id=1, source_target_pairs={{4,0},{8,4},{12,8},{16,12},{20,16},{24,20},{28,24},{5,1},{9,5},{13... | collective-permute-start | bytes 903176 | tf_op jit(solution)/shard_map/ppermute | solution.py:23
  56.9 1.9 %collective-permute-start = (bf16[64,8,294]{2,1,0:T(8,128)(2,1)S(1)}, bf16[64,8,294]{2,1,0:T(8,128)(2,1)S(1)}, u32[]{:S(2)}, u32[]{:S(2)}) collective-permute-start(bf16[64,8,294]{2,1,0:T(8,128)(2,1)S(1)} %bitcast.80), channel_id=1, source_target_pairs={{0,4},{4,8},{8,12},{12,16},{16,20},{20,24},{24,28},{1,5},{5,9},{9,... | collective-permute-start | bytes 903176 | tf_op jit(solution)/shard_map/ppermute | solution.py:21
  58.8 3.0 %fusion.51 = bf16[8,294,1]{1,0,2:T(8,128)(2,1)S(1)} fusion(bf16[16,294,294]{2,0,1:T(8,128)(2,1)} %param.14, bf16[16,8,294]{2,1,0:T(8,128)(2,1)S(1)} %reshape.47), kind=kOutput, calls=%fused_computation.31 | convolution fusion | flops 22129968 | bytes 2845920 | tf_op jit(solution)/shard_map/dot_general | solution.py:105
  61.9 1.3 %fusion.6 = f32[2,8,8,294]{3,1,2,0:T(8,128)} fusion(bf16[8,294,294]{2,0,1:T(8,128)(2,1)S(1)} %copy-done, bf16[8,294,1]{1,0,2:T(8,128)(2,1)S(1)} %fusion.51, bf16[2,294,294]{2,0,1:T(2,128)(2,1)S(1)} %constant_dynamic-slice_fusion), kind=kOutput, calls=%fused_computation.9 | convolution fusion | flops 24898272 | bytes 1883952 | tf_op jit(solution)/shard_map/jnw,kwv->jknv/dot_general | solution.py:117
  63.2 0.3 concatenate.23
  63.5 0.3 concatenate.24
  63.8 5.7 %collective-permute-done = bf16[64,8,294]{2,1,0:T(8,128)(2,1)S(1)} collective-permute-done((bf16[64,8,294]{2,1,0:T(8,128)(2,1)S(1)}, bf16[64,8,294]{2,1,0:T(8,128)(2,1)S(1)}, u32[]{:S(2)}, u32[]{:S(2)}) %collective-permute-start) | collective-permute-done | bytes 301088 | tf_op jit(solution)/shard_map/ppermute | solution.py:21
  69.4 0.3 concatenate.22
  69.8 0.6 convolution_convert_fusion
  70.4 0.8 %copy.14 = bf16[256,2352]{1,0:T(8,128)(2,1)S(1)} copy(bf16[256,2352]{0,1:T(8,128)(2,1)S(1)} %convolution_convert_fusion) | data formatting | bytes 2408448 | tf_op jit(solution)/shard_map/convert_element_type | solution.py:47
  71.3 2.0 %reshape.43 = bf16[16,16,8,294]{3,2,1,0:T(8,128)(2,1)S(1)} reshape(bf16[256,2352]{1,0:T(8,128)(2,1)S(1)} %copy.14) | data formatting | bytes 2408448 | tf_op jit(solution)/shard_map/reshape | solution.py:48
  73.2 4.4 %fusion.27 = bf16[16,8,294]{2,1,0:T(8,128)(2,1)} fusion(f32[16,8,294]{2,1,0:T(8,128)S(1)} %bitcast.82, bf16[16,294,294]{2,0,1:T(8,128)(2,1)} %param.14, bf16[16,16,8,294]{3,2,1,0:T(8,128)(2,1)S(1)} %reshape.43), kind=kOutput, calls=%fused_computation.22 | convolution fusion | flops 354117120 | bytes 4195968 | tf_op jit(solution)/shard_map/dot_general | solution.py:50
  (26 shorter events, 0.1 us)
Async XLA Ops:
  0.0 3.8 %copy-start.1 = (bf16[16,8,294]{2,1,0:T(8,128)(2,1)S(1)}, bf16[16,8,294]{2,1,0:T(8,128)(2,1)}, u32[]{:S(2)}) copy-start(bf16[16,8,294]{2,1,0:T(8,128)(2,1)} %param.8) | copy-start | bytes 225796
  0.0 8.4 %copy-start.4 = (s32[16,189]{1,0:T(8,128)S(1)}, s32[16,189]{1,0:T(8,128)}, u32[]{:S(2)}) copy-start(s32[16,189]{1,0:T(8,128)} %param.10) | copy-start | bytes 36292
  0.0 8.4 %copy-start.3 = (s32[16,189]{1,0:T(8,128)S(1)}, s32[16,189]{1,0:T(8,128)}, u32[]{:S(2)}) copy-start(s32[16,189]{1,0:T(8,128)} %param.9) | copy-start | bytes 36292
  0.0 12.9 %copy-start = (bf16[8,294,294]{2,0,1:T(8,128)(2,1)S(1)}, bf16[8,294,294]{2,0,1:T(8,128)(2,1)}, u32[]{:S(2)}) copy-start(bf16[8,294,294]{2,0,1:T(8,128)(2,1)} %param.15) | copy-start | bytes 4148932
  2.1 11.3 %copy-start.9 = (u32[32]{0:T(128)S(1)}, u32[32]{0:T(128)}, u32[]{:S(2)}) copy-start(u32[32]{0:T(128)} %constant.76) | copy-start | bytes 388
  2.1 11.9 %copy-start.8 = (u32[32]{0:T(128)S(1)}, u32[32]{0:T(128)}, u32[]{:S(2)}) copy-start(u32[32]{0:T(128)} %constant.71) | copy-start | bytes 388
  2.1 7.8 %collective-permute-start.2 = (bf16[2,8,294]{2,1,0:T(8,128)(2,1)S(1)}, bf16[2,8,294]{2,1,0:T(8,128)(2,1)S(1)}, u32[]{:S(2)}, u32[]{:S(2)}) collective-permute-start(bf16[2,8,294]{2,1,0:T(8,128)(2,1)S(1)} %fusion.35), channel_id=1, source_target_pairs={{0,1},{1,0},{2,3},{3,2},{4,5},{5,4},{6,7},{7,6},{8,9},{9,8},{10,11... | collective-permute-start | bytes 28232 | tf_op jit(solution)/shard_map/ppermute | solution.py:10
  4.6 49.7 %all-to-all-start = ((bf16[4,16,8,294]{3,2,1,0:T(8,128)(2,1)}), bf16[4,16,8,294]{3,2,1,0:T(8,128)(2,1)S(1)}, u32[]{:S(2)}, u32[]{:S(2)}) async-start(bf16[4,16,8,294]{3,2,1,0:T(8,128)(2,1)} %stack.2), calls=%async_computation | async-start | bytes 786432 | tf_op jit(solution)/shard_map/all_to_all | solution.py:113
  9.9 43.7 %copy-start.5 = (s32[1,189]{1,0:T(1,128)S(1)}, s32[1,189]{1,0:T(1,128)}, u32[]{:S(2)}) copy-start(s32[1,189]{1,0:T(1,128)} %param.11) | copy-start | bytes 2272
  9.9 43.7 %copy-start.6 = (s32[1,189]{1,0:T(1,128)S(1)}, s32[1,189]{1,0:T(1,128)}, u32[]{:S(2)}) copy-start(s32[1,189]{1,0:T(1,128)} %param.12) | copy-start | bytes 2272
  10.0 10.9 %collective-permute-start.3 = (bf16[4,8,294]{2,1,0:T(8,128)(2,1)S(1)}, bf16[4,8,294]{2,1,0:T(8,128)(2,1)S(1)}, u32[]{:S(2)}, u32[]{:S(2)}) collective-permute-start(bf16[4,8,294]{2,1,0:T(8,128)(2,1)S(1)} %maximum_select_fusion.2), channel_id=1, source_target_pairs={{0,2},{1,3},{2,0},{3,1},{4,6},{5,7},{6,4},{7,5},{8,10},{9,11},{10,... | collective-permute-start | bytes 56456 | tf_op jit(solution)/shard_map/ppermute | solution.py:10
  54.3 9.2 %collective-permute-start.1 = (bf16[64,8,294]{2,1,0:T(8,128)(2,1)S(1)}, bf16[64,8,294]{2,1,0:T(8,128)(2,1)S(1)}, u32[]{:S(2)}, u32[]{:S(2)}) collective-permute-start(bf16[64,8,294]{2,1,0:T(8,128)(2,1)S(1)} %bitcast.79), channel_id=1, source_target_pairs={{4,0},{8,4},{12,8},{16,12},{20,16},{24,20},{28,24},{5,1},{9,5},{13... | collective-permute-start | bytes 903176 | tf_op jit(solution)/shard_map/ppermute | solution.py:23
  56.9 12.5 %collective-permute-start = (bf16[64,8,294]{2,1,0:T(8,128)(2,1)S(1)}, bf16[64,8,294]{2,1,0:T(8,128)(2,1)S(1)}, u32[]{:S(2)}, u32[]{:S(2)}) collective-permute-start(bf16[64,8,294]{2,1,0:T(8,128)(2,1)S(1)} %bitcast.80), channel_id=1, source_target_pairs={{0,4},{4,8},{8,12},{12,16},{16,20},{20,24},{24,28},{1,5},{5,9},{9,... | collective-permute-start | bytes 903176 | tf_op jit(solution)/shard_map/ppermute | solution.py:21
  63.2 6.6 %copy-start.7 = (bf16[16,16,192]{2,1,0:T(8,128)(2,1)S(1)}, bf16[16,16,192]{2,1,0:T(8,128)(2,1)}, u32[]{:S(2)}) copy-start(bf16[16,16,192]{2,1,0:T(8,128)(2,1)} %fusion.21) | copy-start | bytes 294916
  71.2 2.0 %copy-start.2 = (f32[2,8,8,294]{3,1,2,0:T(8,128)S(1)}, f32[2,8,8,294]{3,1,2,0:T(8,128)}, u32[]{:S(2)}) copy-start(f32[2,8,8,294]{3,1,2,0:T(8,128)} %fusion.6) | copy-start | bytes 451588
